TPU v7x, 256 devices: a whole 4x4x8 slice. The times are simulated.
256 devices in a mesh: group: 4 (over y), shard: 64 (over x, z, core).
Axes of the slice: x: 4, y: 4, z: 8, core: 2. Of those that a mesh axis runs over, the one named last changes fastest.
Arguments:
- activations: bfloat16 [4, 128, 256, 1024], P('group', 'shard'), may hold values from -7 to 7
- out_grad: bfloat16 [4, 128, 256, 1024], P('group', None, 'shard'), may hold values from -1.5 to 1.5
- embedding: bfloat16 [512, 1024], replicated, may hold values from -6 to 6
- counts: int32 [4, 8], P('group'), may hold values from 0 to 256, as said below
- offsets: int32 [4, 8], P('group'), may hold values from 0 to 8, as said below
- layout: int32 [4, 256], P('group'), may hold values from 0 to 511
Outputs:
- input_grad: bfloat16 [4, 128, 256, 1024], P('group', 'shard')
- embedding_grad: float32 [512, 1024], P('group')
Inputs may be any that keep to these rules, and one draw needn't show every extreme that they name: `counts`: A used session slot holds 19 to 256 electrodes; slots after the used ones hold 0. `offsets`: used session slots come first; the first starts at block 0 and each next one where the previous ends, a session taking ceil(count / 32) blocks, all sessions together exactly 8 blocks; unused slots hold 8.
All inputs are finite; a program needn't handle non-finite values.
Results may differ from a plain program's by a relative error of at most 0.012.
The roundings to bfloat16 on the way count: a program that leaves them out, or rounds other values in their place, can miss the bound.
Values may be sent and summed in bfloat16 or wider, within the bound.
A program may use at most 64 MiB of HBM per device.

v0:
```python
import math
import jax
import jax.numpy as jnp
from jax import lax
from jax.sharding import PartitionSpec as P

HEADS = 16
BLOCK = 32


def product(form, left, right):
    return jnp.einsum(form, left, right, preferred_element_type=jnp.float32)


def attend(values, allowed):
    length = values.shape[0]
    head_split = values.reshape(length, HEADS, -1)
    score_scale = 0.5 / math.sqrt(head_split.shape[-1])
    scores = product("qhd,khd->hqk", head_split, head_split) * score_scale
    scores = jnp.where(allowed[None], scores, -1e30)
    row_max = jnp.max(scores, axis=-1, keepdims=True)
    exponent = jnp.exp(scores - row_max)
    weights = (exponent / jnp.sum(exponent, axis=-1, keepdims=True)).astype(jnp.bfloat16)
    attended = product("hqk,khd->qhd", weights, head_split)
    return (head_split, weights, attended)


def attend_back(values, allowed, cotangent):
    head_split, weights, attended = attend(values, allowed)
    length = values.shape[0]
    score_scale = 0.5 / math.sqrt(head_split.shape[-1])
    grad_heads = cotangent.reshape(length, HEADS, -1)
    row_delta = jnp.sum(grad_heads.astype(jnp.float32) * attended, axis=-1)
    grad_weights = product("qhd,khd->hqk", grad_heads, head_split)
    grad_scores = (
        weights.astype(jnp.float32) * (grad_weights - jnp.transpose(row_delta)[:, :, None])
    ).astype(jnp.bfloat16)
    grad_values = score_scale * (
        product("hqk,khd->qhd", grad_scores, head_split)
        + product("hqk,qhd->khd", grad_scores, head_split)
    )
    grad_values = grad_values + product("hqk,qhd->khd", weights, grad_heads)
    return grad_values.reshape(length, -1)


def session_pairs(counts, offsets, electrodes):
    slot_index = jnp.arange(electrodes, dtype=jnp.int32)
    block_index = slot_index // BLOCK
    member = (offsets[None, :] <= block_index[:, None]).astype(jnp.int32)
    session = jnp.sum(member, axis=1) - 1
    chosen = (jnp.arange(offsets.shape[0], dtype=jnp.int32)[None, :] == session[:, None]).astype(
        jnp.int32
    )
    first_slot = jnp.sum(chosen * offsets[None, :], axis=1) * BLOCK
    live_count = jnp.sum(chosen * counts[None, :], axis=1)
    is_live = slot_index - first_slot < live_count
    return (session[:, None] == session[None, :]) & is_live[None, :]


def body(activations, out_grad, embedding, counts, offsets, layout):
    local_in = activations[0]
    electrodes = local_in.shape[1]
    templates = embedding.shape[0]
    allowed = session_pairs(counts[0], offsets[0], electrodes)
    onehot = (layout[0][:, None] == jnp.arange(templates, dtype=jnp.int32)[None, :]).astype(
        jnp.bfloat16
    )
    layout_rows = jnp.dot(onehot, embedding, preferred_element_type=jnp.float32)
    embedded = (local_in.astype(jnp.float32) + layout_rows[None]).astype(jnp.bfloat16)

    def spatial(values):
        return (
            values.astype(jnp.float32) + attend(values, allowed)[2].reshape(electrodes, -1)
        ).astype(jnp.bfloat16)

    mixed = lax.map(spatial, embedded)
    gathered = lax.all_to_all(mixed[None], "shard", split_axis=2, concat_axis=1, tiled=True)
    patches = gathered.shape[1]
    full_mask = jnp.ones((patches, patches), dtype=bool)

    def temporal(couple):
        values, cotangent = couple
        return (cotangent.astype(jnp.float32) + attend_back(values, full_mask, cotangent)).astype(
            jnp.bfloat16
        )

    mixed_grad = lax.map(
        temporal, (jnp.moveaxis(gathered[0], 1, 0), jnp.moveaxis(out_grad[0], 1, 0))
    )
    returned = lax.all_to_all(
        jnp.moveaxis(mixed_grad, 0, 1)[None], "shard", split_axis=1, concat_axis=2, tiled=True
    )

    def spatial_back(couple):
        values, cotangent = couple
        return cotangent.astype(jnp.float32) + attend_back(values, allowed, cotangent)

    full_grad = lax.map(spatial_back, (embedded, returned[0]))
    input_grad = full_grad.astype(jnp.bfloat16)[None]
    electrode_grad = jnp.sum(full_grad, axis=0)
    shards = lax.axis_size("shard")
    groups = lax.axis_size("group")
    width = local_in.shape[2]
    pieces = jnp.transpose(electrode_grad).astype(jnp.bfloat16)
    pieces = pieces.reshape(shards, width // shards, electrodes)
    arrived = lax.all_to_all(pieces, "shard", split_axis=0, concat_axis=0, tiled=True)
    own_columns = jnp.sum(arrived.astype(jnp.float32), axis=0)
    column_table = jnp.dot(
        own_columns.astype(jnp.bfloat16), onehot, preferred_element_type=jnp.float32
    )
    own_rows = templates // groups
    column_table = column_table.reshape(width // shards, groups, own_rows)
    from_groups = lax.all_to_all(
        jnp.moveaxis(column_table, 1, 0), "group", split_axis=0, concat_axis=0, tiled=True
    )
    own_part = jnp.sum(from_groups, axis=0)
    gathered_table = lax.all_gather(own_part, "shard", axis=0, tiled=True)
    table_grad = jnp.transpose(gathered_table)
    return (input_grad, table_grad)


def solution(mesh):
    placed = (
        P("group", "shard", None, None),
        P("group", None, "shard", None),
        P(),
        P("group", None),
        P("group", None),
        P("group", None),
    )
    return jax.shard_map(
        body,
        mesh=mesh,
        in_specs=placed,
        out_specs=(P("group", "shard", None, None), P("group", None)),
        check_vma=False,
    )
```

profile of v0, /device:TPU:1, one launch (start us, length us, event | category | flops | bytes accessed | tf_op | source)
XLA Modules:
  0.0 249.8 jit_solution(14660771344484138781)
XLA Ops:
  0.7 0.8 convert_reduce_fusion
  1.5 1.5 copy.80
  3.0 0.8 select_reduce_fusion.1
  3.8 1.3 fusion.39
  5.3 14.4 %while.33 = (s32[]{:T(128)}, bf16[2,256,1024]{1,2,0:T(8,128)(2,1)}, bf16[2,256,1024]{1,2,0:T(8,128)(2,1)S(1)}, s32[256]{0:T(256)S(1)}, pred[256]{0:T(512)(128)(4,1)S(1)}, /*index=5*/s32[]{:T(128)}) while((s32[]{:T(128)}, bf16[2,256,1024]{1,2,0:T(8,128)(2,1)}, bf16[2,256,1024]{1,2,0:T(8,128)(2,1)S(1)}, s32[256]{0:T(256)S(1)}, ...), condition=%wide.region_6.7_spmd.clone, body=%wide.region_3.6_spmd.clone.sunk | while | flops 275644672 | bytes 13797193 | solution.py:76
  5.5 3.4 %fusion.140 = (f32[16,256]{1,0:T(8,128)S(1)}, f32[16,256,256]{1,2,0:T(8,128)}) fusion(pred[256,256]{0,1:T(8,128)(4,1)S(1)} %compare_and_fusion.4, bf16[256,16,64]{0,2,1:T(8,128)(2,1)S(1)} %bitcast.190), kind=kOutput, calls=%fused_computation.86.clone.1 | convolution fusion | flops 138412288 | bytes 4800512 | tf_op jit(solution)/shard_map/while/body/eval_jaxpr/sub | solution.py:22
  8.9 2.7 %fusion.141 = f32[16,64,256]{2,1,0:T(8,128)S(1)} fusion(bf16[256,16,64]{0,2,1:T(8,128)(2,1)S(1)} %bitcast.191, f32[16,256,256]{1,2,0:T(8,128)} %get-tuple-element.283, f32[16,256]{1,0:T(8,128)S(1)} %get-tuple-element.284), kind=kOutput, calls=%fused_computation.30.clone.1 | convolution fusion | flops 136314880 | bytes 5783552 | tf_op jit(solution)/shard_map/while/body/eval_jaxpr/hqk,khd->qhd/dot_general | solution.py:12
  11.6 0.9 constant_dynamic-update-slice_fusion.7
  12.7 3.4 %fusion.140 = (f32[16,256]{1,0:T(8,128)S(1)}, f32[16,256,256]{1,2,0:T(8,128)}) fusion(pred[256,256]{0,1:T(8,128)(4,1)S(1)} %compare_and_fusion.4, bf16[256,16,64]{0,2,1:T(8,128)(2,1)S(1)} %bitcast.190), kind=kOutput, calls=%fused_computation.86.clone.1 | convolution fusion | flops 138412288 | bytes 4800512 | tf_op jit(solution)/shard_map/while/body/eval_jaxpr/sub | solution.py:22
  16.1 2.7 %fusion.141 = f32[16,64,256]{2,1,0:T(8,128)S(1)} fusion(bf16[256,16,64]{0,2,1:T(8,128)(2,1)S(1)} %bitcast.191, f32[16,256,256]{1,2,0:T(8,128)} %get-tuple-element.283, f32[16,256]{1,0:T(8,128)S(1)} %get-tuple-element.284), kind=kOutput, calls=%fused_computation.30.clone.1 | convolution fusion | flops 136314880 | bytes 5783552 | tf_op jit(solution)/shard_map/while/body/eval_jaxpr/hqk,khd->qhd/dot_general | solution.py:12
  18.8 0.9 constant_dynamic-update-slice_fusion.7
  19.7 3.7 %copy.82 = bf16[2,256,1024]{2,0,1:T(2,128)(2,1)} copy(bf16[2,256,1024]{1,2,0:T(8,128)(2,1)} %get-tuple-element.73) | data formatting | bytes 2097152 | tf_op jit(solution)/shard_map/while | solution.py:76
  23.5 13.0 %all-to-all-start = ((bf16[1,2,256,1024]{3,1,0,2:T(2,128)(2,1)}), bf16[1,2,256,1024]{3,1,0,2:T(2,128)(2,1)S(1)}, u32[]{:S(2)}, u32[]{:S(2)}) async-start(bf16[1,2,256,1024]{3,1,0,2:T(2,128)(2,1)} %bitcast.195), calls=%async_computation | async-start | bytes 2097152 | tf_op jit(solution)/shard_map/all_to_all | solution.py:77
  36.5 2.7 %copy.79 = bf16[1,128,4,1024]{1,3,2,0:T(8,128)(2,1)} copy(bf16[1,128,4,1024]{3,2,1,0:T(4,128)(2,1)} %param.13) | data formatting | bytes 2097152 | tf_op args[1]
  39.1 25.8 %all-to-all-done = bf16[1,2,256,1024]{3,1,0,2:T(2,128)(2,1)S(1)} async-done(((bf16[1,2,256,1024]{3,1,0,2:T(2,128)(2,1)}), bf16[1,2,256,1024]{3,1,0,2:T(2,128)(2,1)S(1)}, u32[]{:S(2)}, u32[]{:S(2)}) %all-to-all-start) | async-done | bytes 1048608 | tf_op jit(solution)/shard_map/all_to_all | solution.py:77
  65.0 1.5 copy.83
  66.5 2.7 %copy.84 = bf16[4,128,1024]{1,2,0:T(8,128)(2,1)} copy(bf16[4,128,1024]{2,0,1:T(4,128)(2,1)} %bitcast.197) | data formatting | bytes 2097152 | tf_op jit(solution)/shard_map/while | solution.py:87
  69.2 26.1 %while.32 = (s32[]{:T(128)}, bf16[4,128,1024]{1,2,0:T(8,128)(2,1)}, bf16[4,128,1024]{1,2,0:T(8,128)(2,1)}, bf16[4,128,1024]{1,2,0:T(8,128)(2,1)}, s32[]{:T(128)}) while((s32[]{:T(128)}, bf16[4,128,1024]{1,2,0:T(8,128)(2,1)}, bf16[4,128,1024]{1,2,0:T(8,128)(2,1)}, bf16[4,128,1024]{1,2,0:T(8,128)(2,1)}, s32[]{:T(128)}) %tuple.88), condition=%wide.region_11.12_spmd, body=%wide.region_7.11_spmd.sunk | while | flops 204863616 | bytes 12616257 | solution.py:87
  69.2 1.1 constant_dynamic-slice_fusion.8
  70.3 1.5 fusion.132
  71.7 1.3 divide_convert_fusion.7
  74.9 0.8 constant_dynamic-update-slice_fusion.6
  75.7 1.1 constant_dynamic-slice_fusion.8
  76.8 1.5 fusion.132
  78.3 1.3 divide_convert_fusion.7
  81.5 0.8 constant_dynamic-update-slice_fusion.6
  82.2 1.1 constant_dynamic-slice_fusion.8
  83.3 1.5 fusion.132
  84.8 1.3 divide_convert_fusion.7
  88.0 0.8 constant_dynamic-update-slice_fusion.6
  88.7 1.1 constant_dynamic-slice_fusion.8
  89.8 1.5 fusion.132
  91.3 1.3 divide_convert_fusion.7
  94.5 0.8 constant_dynamic-update-slice_fusion.6
  95.3 2.7 %copy.85 = bf16[4,128,1024]{2,0,1:T(4,128)(2,1)} copy(bf16[4,128,1024]{1,2,0:T(8,128)(2,1)} %get-tuple-element.74) | data formatting | bytes 2097152 | tf_op jit(solution)/shard_map/while | solution.py:87
  98.0 6.2 %all-to-all-start.1 = ((bf16[1,128,4,1024]{3,2,0,1:T(4,128)(2,1)}), bf16[1,128,4,1024]{3,2,0,1:T(4,128)(2,1)S(1)}, u32[]{:S(2)}, u32[]{:S(2)}) async-start(bf16[1,128,4,1024]{3,2,0,1:T(4,128)(2,1)} %bitcast.196), calls=%async_computation.1 | async-start | bytes 2097152 | tf_op jit(solution)/shard_map/all_to_all | solution.py:90
  104.2 28.5 %all-to-all-done.1 = bf16[1,128,4,1024]{3,2,0,1:T(4,128)(2,1)S(1)} async-done(((bf16[1,128,4,1024]{3,2,0,1:T(4,128)(2,1)}), bf16[1,128,4,1024]{3,2,0,1:T(4,128)(2,1)S(1)}, u32[]{:S(2)}, u32[]{:S(2)}) %all-to-all-start.1) | async-done | bytes 1048608 | tf_op jit(solution)/shard_map/all_to_all | solution.py:90
  132.7 2.1 copy.86
  134.8 3.6 %copy.87 = bf16[2,256,1024]{1,2,0:T(8,128)(2,1)} copy(bf16[2,256,1024]{2,0,1:T(2,128)(2,1)} %bitcast.198) | data formatting | bytes 2097152
  138.4 23.5 %while.34 = (s32[]{:T(128)}, f32[2,256,1024]{1,2,0:T(8,128)}, bf16[2,256,1024]{1,2,0:T(8,128)(2,1)}, bf16[2,256,1024]{1,2,0:T(8,128)(2,1)S(1)}, s32[256]{0:T(256)S(1)}, /*index=5*/pred[256]{0:T(512)(128)(4,1)S(1)}, s32[]{:T(128)}) while((s32[]{:T(128)}, f32[2,256,1024]{1,2,0:T(8,128)}, bf16[2,256,1024]{1,2,0:T(8,128)(2,1)}, ...), condition=%wide.region_16.17_spmd.clone, body=%wide.region_12.16_spmd.clone.sunk | while | flops 818016512 | bytes 37422928 | solution.py:98
  138.4 1.1 constant_dynamic-slice_fusion.10
  139.6 3.4 %fusion.154 = (f32[16,256]{1,0:T(8,128)S(1)}, f32[16,256,256]{1,2,0:T(8,128)}) fusion(pred[256,256]{0,1:T(8,128)(4,1)S(1)} %compare_and_fusion.5, bf16[256,16,64]{0,2,1:T(8,128)(2,1)S(1)} %bitcast.174), kind=kOutput, calls=%fused_computation.87.clone.1 | convolution fusion | flops 138412288 | bytes 4800512 | tf_op jit(solution)/shard_map/while/body/eval_jaxpr/sub | solution.py:22
  143.1 2.6 %divide_convert_fusion.9 = bf16[16,256,256]{1,2,0:T(8,128)(2,1)S(1)} fusion(f32[16,256,256]{1,2,0:T(8,128)} %get-tuple-element.292, f32[16,256]{1,0:T(8,128)S(1)} %get-tuple-element.293), kind=kLoop, calls=%fused_computation.42.clone.1 | loop fusion | flops 2097152 | bytes 6307840 | tf_op jit(solution)/shard_map/while/body/eval_jaxpr/convert_element_type | solution.py:23
  145.7 0.5 fusion.155
  146.2 0.8 multiply_convert_fusion.2
  147.5 0.8 fusion.157
  148.3 0.8 convolution_add_fusion.7
  149.0 1.1 constant_dynamic-update-slice_fusion.8
  150.1 1.1 constant_dynamic-slice_fusion.10
  151.4 3.4 %fusion.154 = (f32[16,256]{1,0:T(8,128)S(1)}, f32[16,256,256]{1,2,0:T(8,128)}) fusion(pred[256,256]{0,1:T(8,128)(4,1)S(1)} %compare_and_fusion.5, bf16[256,16,64]{0,2,1:T(8,128)(2,1)S(1)} %bitcast.174), kind=kOutput, calls=%fused_computation.87.clone.1 | convolution fusion | flops 138412288 | bytes 4800512 | tf_op jit(solution)/shard_map/while/body/eval_jaxpr/sub | solution.py:22
  154.8 2.6 %divide_convert_fusion.9 = bf16[16,256,256]{1,2,0:T(8,128)(2,1)S(1)} fusion(f32[16,256,256]{1,2,0:T(8,128)} %get-tuple-element.292, f32[16,256]{1,0:T(8,128)S(1)} %get-tuple-element.293), kind=kLoop, calls=%fused_computation.42.clone.1 | loop fusion | flops 2097152 | bytes 6307840 | tf_op jit(solution)/shard_map/while/body/eval_jaxpr/convert_element_type | solution.py:23
  157.9 0.8 multiply_convert_fusion.2
  159.3 0.8 fusion.157
  160.0 0.8 convolution_add_fusion.7
  160.8 1.1 constant_dynamic-update-slice_fusion.8
  161.9 2.7 %reduce_sum.105 = bf16[256,1024]{0,1:T(8,128)(2,1)} reduce(f32[2,256,1024]{1,2,0:T(8,128)} %get-tuple-element.75, f32[]{:T(128)} %constant.80.clone.1), dimensions={0}, to_apply=%region_17.18 | reduce | flops 262144 | bytes 2621444 | tf_op jit(solution)/shard_map/reduce_sum | solution.py:100
  164.6 6.2 %all-to-all-start.2 = ((bf16[64,16,256]{2,1,0:T(8,128)(2,1)}), bf16[64,16,256]{2,1,0:T(8,128)(2,1)S(1)}, u32[]{:S(2)}, u32[]{:S(2)}) async-start(bf16[64,16,256]{2,1,0:T(8,128)(2,1)} %bitcast.24), calls=%async_computation.2 | async-start | bytes 1048576 | tf_op jit(solution)/shard_map/all_to_all | solution.py:106
  170.8 17.3 %all-to-all-done.2 = bf16[64,16,256]{2,1,0:T(8,128)(2,1)S(1)} async-done(((bf16[64,16,256]{2,1,0:T(8,128)(2,1)}), bf16[64,16,256]{2,1,0:T(8,128)(2,1)S(1)}, u32[]{:S(2)}, u32[]{:S(2)}) %all-to-all-start.2) | async-done | bytes 524320 | tf_op jit(solution)/shard_map/all_to_all | solution.py:106
  188.2 0.9 convolution_bitcast_fusion.2
  189.1 4.2 %all-to-all-start.3 = ((f32[4,16,128]{2,1,0:T(8,128)}), f32[4,16,128]{2,1,0:T(8,128)S(1)}, u32[]{:S(2)}, u32[]{:S(2)}) async-start(f32[4,16,128]{2,1,0:T(8,128)} %convolution_bitcast_fusion.2), calls=%async_computation.3 | async-start | bytes 65536 | tf_op jit(solution)/shard_map/all_to_all | solution.py:113
  193.3 2.5 %copy.88 = bf16[2,256,1024]{2,1,0:T(8,128)(2,1)} copy(f32[2,256,1024]{1,2,0:T(8,128)} %get-tuple-element.75) | data formatting | bytes 3145728 | tf_op jit(solution)/shard_map/while | solution.py:98
  195.8 1.8 all-to-all-done.3
  197.6 51.2 %all_gather.3 = f32[1024,128]{1,0:T(8,128)S(1)} all-gather(f32[16,128]{1,0:T(8,128)S(1)} %reduce_sum.107), channel_id=1, replica_groups=mesh['group'=4,'shard'=64] {'shard'}, dimensions={0}, use_global_device_ids=true | all-gather | bytes 532480 | tf_op jit(solution)/shard_map/all_gather | solution.py:117
  248.8 1.0 copy.89
  (43 shorter events, 9.8 us)
Async XLA Ops:
  0.6 3.1 %copy-start = (bf16[512,1024]{1,0:T(8,128)(2,1)S(1)}, bf16[512,1024]{1,0:T(8,128)(2,1)}, u32[]{:S(2)}) copy-start(bf16[512,1024]{1,0:T(8,128)(2,1)} %param.14) | copy-start | bytes 3145732
  23.5 41.5 %all-to-all-start = ((bf16[1,2,256,1024]{3,1,0,2:T(2,128)(2,1)}), bf16[1,2,256,1024]{3,1,0,2:T(2,128)(2,1)S(1)}, u32[]{:S(2)}, u32[]{:S(2)}) async-start(bf16[1,2,256,1024]{3,1,0,2:T(2,128)(2,1)} %bitcast.195), calls=%async_computation | async-start | bytes 2097152 | tf_op jit(solution)/shard_map/all_to_all | solution.py:77
  98.0 34.7 %all-to-all-start.1 = ((bf16[1,128,4,1024]{3,2,0,1:T(4,128)(2,1)}), bf16[1,128,4,1024]{3,2,0,1:T(4,128)(2,1)S(1)}, u32[]{:S(2)}, u32[]{:S(2)}) async-start(bf16[1,128,4,1024]{3,2,0,1:T(4,128)(2,1)} %bitcast.196), calls=%async_computation.1 | async-start | bytes 2097152 | tf_op jit(solution)/shard_map/all_to_all | solution.py:90
  161.9 26.3 %copy-start.1 = (s32[1,256]{1,0:T(1,128)S(1)}, s32[1,256]{1,0:T(1,128)}, u32[]{:S(2)}) copy-start(s32[1,256]{1,0:T(1,128)} %param.17) | copy-start | bytes 3076
  164.6 23.5 %all-to-all-start.2 = ((bf16[64,16,256]{2,1,0:T(8,128)(2,1)}), bf16[64,16,256]{2,1,0:T(8,128)(2,1)S(1)}, u32[]{:S(2)}, u32[]{:S(2)}) async-start(bf16[64,16,256]{2,1,0:T(8,128)(2,1)} %bitcast.24), calls=%async_computation.2 | async-start | bytes 1048576 | tf_op jit(solution)/shard_map/all_to_all | solution.py:106
  189.1 8.5 %all-to-all-start.3 = ((f32[4,16,128]{2,1,0:T(8,128)}), f32[4,16,128]{2,1,0:T(8,128)S(1)}, u32[]{:S(2)}, u32[]{:S(2)}) async-start(f32[4,16,128]{2,1,0:T(8,128)} %convolution_bitcast_fusion.2), calls=%async_computation.3 | async-start | bytes 65536 | tf_op jit(solution)/shard_map/all_to_all | solution.py:113
where the time goes:
time: 251 us; the launch traced here: 250 us
  waiting for transfers between devices  73.4 us (29%)
  blocking collectives  51.2 us (20%)
  matrix products  41.2 us (16%)
  local copies, waits for them, and re-layouts  30.6 us (12%)
  starting transfers between devices  29.5 us (12%)
  other arithmetic  22.9 us (9%)
    all_gather x1, blocking collectives, body(): gathered_table = lax.all_gather(own_part, 'shard', axis=0, tiled=True)  51.2 us
    all_to_all x1, waiting for transfers between devices, body(): lax.all_to_all(jnp.moveaxis(mixed_grad, 0, 1)[None], 'shard', split_axis=...  28.5 us
    all_to_all x1, waiting for transfers between devices, body(): lax.all_to_all(mixed[None], 'shard', split_axis=2, concat_axis=1, tiled=T...  25.8 us
    sub x8, matrix products, attend(): exponent = jnp.exp(scores - row_max)  19.6 us
    dot_general x32, matrix products, product(): return jnp.einsum(form, left, right, preferred_element_type=jnp.float32)  19.4 us
    all_to_all x1, waiting for transfers between devices, body(): lax.all_to_all(pieces, 'shard', split_axis=0, concat_axis=0, tiled=True)  17.3 us
    all_to_all x1, starting transfers between devices, body(): lax.all_to_all(mixed[None], 'shard', split_axis=2, concat_axis=1, tiled=T...  13 us
    convert_element_type x6, other arithmetic, attend(): (exponent / jnp.sum(exponent, axis=-1, keepdims=True)).astype(jnp.bfloat16)  10.6 us
  transfers between devices with their start and end apart: 4, of which 4 were waited for; matrix products, arithmetic and copies ran while one was open for 2% of the time, Pallas kernels for 0%

commit v1 on v0

--- a/solution.py
+++ b/solution.py
@@ -114,7 +114,14 @@
         jnp.moveaxis(column_table, 1, 0), "group", split_axis=0, concat_axis=0, tiled=True
     )
     own_part = jnp.sum(from_groups, axis=0)
-    gathered_table = lax.all_gather(own_part, "shard", axis=0, tiled=True)
+
+    def get_array(load, at_axis):
+        return jnp.concatenate(
+            jax.lax.all_to_all(jnp.stack([load] * jax.lax.axis_size("shard")), "shard", 0, 0),
+            at_axis,
+        )
+
+    gathered_table = get_array(own_part, 0)
     table_grad = jnp.transpose(gathered_table)
     return (input_grad, table_grad)
 

time: 251 us -> 225 us (0.90)
  blocking collectives: 51.2 us -> 8.29 us
  waiting for transfers between devices: 73.4 us -> 86.4 us
  starting transfers between devices: 29.5 us -> 33.1 us
    all_gather x1 -> x0, blocking collectives: 51.2 us -> none  [body(): gathered_table = lax.all_gather(own_part, 'shard', axis=0, tiled=True)]
    all_to_all x1, waiting for transfers between devices: 1.76 us -> 14.7 us  [get_array(): jax.lax.all_to_all(jnp.stack([load] * jax.lax.axis_size('shard')), 'shard...]
    all_to_all x0 -> x1, blocking collectives: none -> 8.29 us  [body(): lax.all_to_all(jnp.moveaxis(column_table, 1, 0), 'group', split_axis=0, c...]
    all_to_all x1, starting transfers between devices: 4.19 us -> 7.72 us  [get_array(): jax.lax.all_to_all(jnp.stack([load] * jax.lax.axis_size('shard')), 'shard...]
where the time goes in v1:
time: 225 us; the launch traced here: 224 us
  waiting for transfers between devices  86.4 us (38%)
  matrix products  40.5 us (18%)
  starting transfers between devices  33.1 us (15%)
  local copies, waits for them, and re-layouts  31.4 us (14%)
  other arithmetic  22.9 us (10%)
  blocking collectives  8.29 us (4%)
    all_to_all x1, waiting for transfers between devices, body(): lax.all_to_all(jnp.moveaxis(mixed_grad, 0, 1)[None], 'shard', split_axis=...  28.5 us
    all_to_all x1, waiting for transfers between devices, body(): lax.all_to_all(mixed[None], 'shard', split_axis=2, concat_axis=1, tiled=T...  25.8 us
    sub x8, matrix products, attend(): exponent = jnp.exp(scores - row_max)  19.6 us
    dot_general x32, matrix products, product(): return jnp.einsum(form, left, right, preferred_element_type=jnp.float32)  19.4 us
    all_to_all x1, waiting for transfers between devices, body(): lax.all_to_all(pieces, 'shard', split_axis=0, concat_axis=0, tiled=True)  17.3 us
    all_to_all x1, waiting for transfers between devices, get_array(): jax.lax.all_to_all(jnp.stack([load] * jax.lax.axis_size('shard')), 'shard...  14.7 us
    all_to_all x1, starting transfers between devices, body(): lax.all_to_all(mixed[None], 'shard', split_axis=2, concat_axis=1, tiled=T...  13 us
    convert_element_type x6, other arithmetic, attend(): (exponent / jnp.sum(exponent, axis=-1, keepdims=True)).astype(jnp.bfloat16)  10.6 us
  transfers between devices with their start and end apart: 4, of which 4 were waited for; matrix products, arithmetic and copies ran while one was open for 2% of the time, Pallas kernels for 0%

profile of v1, /device:TPU:1, one launch (start us, length us, event | category | flops | bytes accessed | tf_op | source)
XLA Modules:
  0.0 223.6 jit_solution(470595126102113410)
XLA Ops:
  0.7 0.8 convert_reduce_fusion
  1.5 1.5 copy.81
  3.0 0.8 select_reduce_fusion.1
  3.8 1.3 fusion.39
  5.3 14.4 %while.33 = (s32[]{:T(128)}, bf16[2,256,1024]{1,2,0:T(8,128)(2,1)}, bf16[2,256,1024]{1,2,0:T(8,128)(2,1)S(1)}, s32[256]{0:T(256)S(1)}, pred[256]{0:T(512)(128)(4,1)S(1)}, /*index=5*/s32[]{:T(128)}) while((s32[]{:T(128)}, bf16[2,256,1024]{1,2,0:T(8,128)(2,1)}, bf16[2,256,1024]{1,2,0:T(8,128)(2,1)S(1)}, s32[256]{0:T(256)S(1)}, ...), condition=%wide.region_6.7_spmd.clone, body=%wide.region_3.6_spmd.clone.sunk | while | flops 275644672 | bytes 13797193 | solution.py:76
  5.5 3.4 %fusion.140 = (f32[16,256]{1,0:T(8,128)S(1)}, f32[16,256,256]{1,2,0:T(8,128)}) fusion(pred[256,256]{0,1:T(8,128)(4,1)S(1)} %compare_and_fusion.4, bf16[256,16,64]{0,2,1:T(8,128)(2,1)S(1)} %bitcast.192), kind=kOutput, calls=%fused_computation.86.clone.1 | convolution fusion | flops 138412288 | bytes 4800512 | tf_op jit(solution)/shard_map/while/body/eval_jaxpr/sub | solution.py:22
  8.9 2.7 %fusion.141 = f32[16,64,256]{2,1,0:T(8,128)S(1)} fusion(bf16[256,16,64]{0,2,1:T(8,128)(2,1)S(1)} %bitcast.193, f32[16,256,256]{1,2,0:T(8,128)} %get-tuple-element.285, f32[16,256]{1,0:T(8,128)S(1)} %get-tuple-element.286), kind=kOutput, calls=%fused_computation.30.clone.1 | convolution fusion | flops 136314880 | bytes 5783552 | tf_op jit(solution)/shard_map/while/body/eval_jaxpr/hqk,khd->qhd/dot_general | solution.py:12
  11.6 0.9 constant_dynamic-update-slice_fusion.7
  12.7 3.4 %fusion.140 = (f32[16,256]{1,0:T(8,128)S(1)}, f32[16,256,256]{1,2,0:T(8,128)}) fusion(pred[256,256]{0,1:T(8,128)(4,1)S(1)} %compare_and_fusion.4, bf16[256,16,64]{0,2,1:T(8,128)(2,1)S(1)} %bitcast.192), kind=kOutput, calls=%fused_computation.86.clone.1 | convolution fusion | flops 138412288 | bytes 4800512 | tf_op jit(solution)/shard_map/while/body/eval_jaxpr/sub | solution.py:22
  16.1 2.7 %fusion.141 = f32[16,64,256]{2,1,0:T(8,128)S(1)} fusion(bf16[256,16,64]{0,2,1:T(8,128)(2,1)S(1)} %bitcast.193, f32[16,256,256]{1,2,0:T(8,128)} %get-tuple-element.285, f32[16,256]{1,0:T(8,128)S(1)} %get-tuple-element.286), kind=kOutput, calls=%fused_computation.30.clone.1 | convolution fusion | flops 136314880 | bytes 5783552 | tf_op jit(solution)/shard_map/while/body/eval_jaxpr/hqk,khd->qhd/dot_general | solution.py:12
  18.8 0.9 constant_dynamic-update-slice_fusion.7
  19.7 3.7 %copy.83 = bf16[2,256,1024]{2,0,1:T(2,128)(2,1)} copy(bf16[2,256,1024]{1,2,0:T(8,128)(2,1)} %get-tuple-element.73) | data formatting | bytes 2097152 | tf_op jit(solution)/shard_map/while | solution.py:76
  23.5 13.0 %all-to-all-start = ((bf16[1,2,256,1024]{3,1,0,2:T(2,128)(2,1)}), bf16[1,2,256,1024]{3,1,0,2:T(2,128)(2,1)S(1)}, u32[]{:S(2)}, u32[]{:S(2)}) async-start(bf16[1,2,256,1024]{3,1,0,2:T(2,128)(2,1)} %bitcast.197), calls=%async_computation | async-start | bytes 2097152 | tf_op jit(solution)/shard_map/all_to_all | solution.py:77
  36.5 2.7 %copy.80 = bf16[1,128,4,1024]{1,3,2,0:T(8,128)(2,1)} copy(bf16[1,128,4,1024]{3,2,1,0:T(4,128)(2,1)} %param.13) | data formatting | bytes 2097152 | tf_op args[1]
  39.1 25.8 %all-to-all-done = bf16[1,2,256,1024]{3,1,0,2:T(2,128)(2,1)S(1)} async-done(((bf16[1,2,256,1024]{3,1,0,2:T(2,128)(2,1)}), bf16[1,2,256,1024]{3,1,0,2:T(2,128)(2,1)S(1)}, u32[]{:S(2)}, u32[]{:S(2)}) %all-to-all-start) | async-done | bytes 1048608 | tf_op jit(solution)/shard_map/all_to_all | solution.py:77
  65.0 1.5 copy.84
  66.5 2.7 %copy.85 = bf16[4,128,1024]{1,2,0:T(8,128)(2,1)} copy(bf16[4,128,1024]{2,0,1:T(4,128)(2,1)} %bitcast.199) | data formatting | bytes 2097152 | tf_op jit(solution)/shard_map/while | solution.py:87
  69.2 26.1 %while.32 = (s32[]{:T(128)}, bf16[4,128,1024]{1,2,0:T(8,128)(2,1)}, bf16[4,128,1024]{1,2,0:T(8,128)(2,1)}, bf16[4,128,1024]{1,2,0:T(8,128)(2,1)}, s32[]{:T(128)}) while((s32[]{:T(128)}, bf16[4,128,1024]{1,2,0:T(8,128)(2,1)}, bf16[4,128,1024]{1,2,0:T(8,128)(2,1)}, bf16[4,128,1024]{1,2,0:T(8,128)(2,1)}, s32[]{:T(128)}) %tuple.89), condition=%wide.region_11.12_spmd, body=%wide.region_7.11_spmd.sunk | while | flops 204863616 | bytes 12616257 | solution.py:87
  69.2 1.1 constant_dynamic-slice_fusion.8
  70.3 1.5 fusion.132
  71.7 1.3 divide_convert_fusion.7
  74.9 0.8 constant_dynamic-update-slice_fusion.6
  75.7 1.1 constant_dynamic-slice_fusion.8
  76.8 1.5 fusion.132
  78.3 1.3 divide_convert_fusion.7
  81.5 0.8 constant_dynamic-update-slice_fusion.6
  82.2 1.1 constant_dynamic-slice_fusion.8
  83.3 1.5 fusion.132
  84.8 1.3 divide_convert_fusion.7
  88.0 0.8 constant_dynamic-update-slice_fusion.6
  88.7 1.1 constant_dynamic-slice_fusion.8
  89.8 1.5 fusion.132
  91.3 1.3 divide_convert_fusion.7
  94.5 0.8 constant_dynamic-update-slice_fusion.6
  95.3 2.7 %copy.86 = bf16[4,128,1024]{2,0,1:T(4,128)(2,1)} copy(bf16[4,128,1024]{1,2,0:T(8,128)(2,1)} %get-tuple-element.74) | data formatting | bytes 2097152 | tf_op jit(solution)/shard_map/while | solution.py:87
  98.0 6.2 %all-to-all-start.1 = ((bf16[1,128,4,1024]{3,2,0,1:T(4,128)(2,1)}), bf16[1,128,4,1024]{3,2,0,1:T(4,128)(2,1)S(1)}, u32[]{:S(2)}, u32[]{:S(2)}) async-start(bf16[1,128,4,1024]{3,2,0,1:T(4,128)(2,1)} %bitcast.198), calls=%async_computation.1 | async-start | bytes 2097152 | tf_op jit(solution)/shard_map/all_to_all | solution.py:90
  104.2 28.5 %all-to-all-done.1 = bf16[1,128,4,1024]{3,2,0,1:T(4,128)(2,1)S(1)} async-done(((bf16[1,128,4,1024]{3,2,0,1:T(4,128)(2,1)}), bf16[1,128,4,1024]{3,2,0,1:T(4,128)(2,1)S(1)}, u32[]{:S(2)}, u32[]{:S(2)}) %all-to-all-start.1) | async-done | bytes 1048608 | tf_op jit(solution)/shard_map/all_to_all | solution.py:90
  132.7 2.1 copy.87
  134.8 3.6 %copy.88 = bf16[2,256,1024]{1,2,0:T(8,128)(2,1)} copy(bf16[2,256,1024]{2,0,1:T(2,128)(2,1)} %bitcast.200) | data formatting | bytes 2097152
  138.4 23.5 %while.34 = (s32[]{:T(128)}, f32[2,256,1024]{1,2,0:T(8,128)}, bf16[2,256,1024]{1,2,0:T(8,128)(2,1)}, bf16[2,256,1024]{1,2,0:T(8,128)(2,1)S(1)}, s32[256]{0:T(256)S(1)}, /*index=5*/pred[256]{0:T(512)(128)(4,1)S(1)}, s32[]{:T(128)}) while((s32[]{:T(128)}, f32[2,256,1024]{1,2,0:T(8,128)}, bf16[2,256,1024]{1,2,0:T(8,128)(2,1)}, ...), condition=%wide.region_16.17_spmd.clone, body=%wide.region_12.16_spmd.clone.sunk | while | flops 818016512 | bytes 37422928 | solution.py:98
  138.4 1.1 constant_dynamic-slice_fusion.10
  139.6 3.4 %fusion.154 = (f32[16,256]{1,0:T(8,128)S(1)}, f32[16,256,256]{1,2,0:T(8,128)}) fusion(pred[256,256]{0,1:T(8,128)(4,1)S(1)} %compare_and_fusion.5, bf16[256,16,64]{0,2,1:T(8,128)(2,1)S(1)} %bitcast.176), kind=kOutput, calls=%fused_computation.87.clone.1 | convolution fusion | flops 138412288 | bytes 4800512 | tf_op jit(solution)/shard_map/while/body/eval_jaxpr/sub | solution.py:22
  143.1 2.6 %divide_convert_fusion.9 = bf16[16,256,256]{1,2,0:T(8,128)(2,1)S(1)} fusion(f32[16,256,256]{1,2,0:T(8,128)} %get-tuple-element.294, f32[16,256]{1,0:T(8,128)S(1)} %get-tuple-element.295), kind=kLoop, calls=%fused_computation.42.clone.1 | loop fusion | flops 2097152 | bytes 6307840 | tf_op jit(solution)/shard_map/while/body/eval_jaxpr/convert_element_type | solution.py:23
  145.7 0.5 fusion.155
  146.2 0.8 multiply_convert_fusion.2
  147.5 0.8 fusion.157
  148.3 0.8 convolution_add_fusion.7
  149.0 1.1 constant_dynamic-update-slice_fusion.8
  150.1 1.1 constant_dynamic-slice_fusion.10
  151.4 3.4 %fusion.154 = (f32[16,256]{1,0:T(8,128)S(1)}, f32[16,256,256]{1,2,0:T(8,128)}) fusion(pred[256,256]{0,1:T(8,128)(4,1)S(1)} %compare_and_fusion.5, bf16[256,16,64]{0,2,1:T(8,128)(2,1)S(1)} %bitcast.176), kind=kOutput, calls=%fused_computation.87.clone.1 | convolution fusion | flops 138412288 | bytes 4800512 | tf_op jit(solution)/shard_map/while/body/eval_jaxpr/sub | solution.py:22
  154.8 2.6 %divide_convert_fusion.9 = bf16[16,256,256]{1,2,0:T(8,128)(2,1)S(1)} fusion(f32[16,256,256]{1,2,0:T(8,128)} %get-tuple-element.294, f32[16,256]{1,0:T(8,128)S(1)} %get-tuple-element.295), kind=kLoop, calls=%fused_computation.42.clone.1 | loop fusion | flops 2097152 | bytes 6307840 | tf_op jit(solution)/shard_map/while/body/eval_jaxpr/convert_element_type | solution.py:23
  157.9 0.8 multiply_convert_fusion.2
  159.3 0.8 fusion.157
  160.0 0.8 convolution_add_fusion.7
  160.8 1.1 constant_dynamic-update-slice_fusion.8
  161.9 2.7 %reduce_sum.105 = bf16[256,1024]{0,1:T(8,128)(2,1)} reduce(f32[2,256,1024]{1,2,0:T(8,128)} %get-tuple-element.75, f32[]{:T(128)} %constant.80.clone.1), dimensions={0}, to_apply=%region_17.18 | reduce | flops 262144 | bytes 2621444 | tf_op jit(solution)/shard_map/reduce_sum | solution.py:100
  164.6 6.2 %all-to-all-start.2 = ((bf16[64,16,256]{2,1,0:T(8,128)(2,1)}), bf16[64,16,256]{2,1,0:T(8,128)(2,1)S(1)}, u32[]{:S(2)}, u32[]{:S(2)}) async-start(bf16[64,16,256]{2,1,0:T(8,128)(2,1)} %bitcast.24), calls=%async_computation.2 | async-start | bytes 1048576 | tf_op jit(solution)/shard_map/all_to_all | solution.py:106
  170.8 17.3 %all-to-all-done.2 = bf16[64,16,256]{2,1,0:T(8,128)(2,1)S(1)} async-done(((bf16[64,16,256]{2,1,0:T(8,128)(2,1)}), bf16[64,16,256]{2,1,0:T(8,128)(2,1)S(1)}, u32[]{:S(2)}, u32[]{:S(2)}) %all-to-all-start.2) | async-done | bytes 524320 | tf_op jit(solution)/shard_map/all_to_all | solution.py:106
  188.5 8.3 %all_to_all.45 = f32[4,16,128]{2,1,0:T(8,128)S(1)} all-to-all(f32[4,16,128]{2,1,0:T(8,128)S(1)} %convolution_bitcast_fusion.2), channel_id=1, replica_groups=mesh['group'=4,'shard'=64] {'group'}, dimensions={0} | all-to-all | bytes 65536 | tf_op jit(solution)/shard_map/all_to_all | solution.py:113
  196.8 0.8 stack.2
  197.6 7.7 %all-to-all-start.4 = ((f32[64,16,128]{2,1,0:T(8,128)}), f32[64,16,128]{2,1,0:T(8,128)S(1)}, u32[]{:S(2)}, u32[]{:S(2)}) async-start(f32[64,16,128]{2,1,0:T(8,128)} %stack.2), calls=%async_computation.4 | async-start | bytes 1048576 | tf_op jit(solution)/shard_map/all_to_all | solution.py:120
  205.3 2.5 %copy.89 = bf16[2,256,1024]{2,1,0:T(8,128)(2,1)} copy(f32[2,256,1024]{1,2,0:T(8,128)} %get-tuple-element.75) | data formatting | bytes 3145728 | tf_op jit(solution)/shard_map/while | solution.py:98
  207.9 14.7 %all-to-all-done.4 = f32[64,16,128]{2,1,0:T(8,128)S(1)} async-done(((f32[64,16,128]{2,1,0:T(8,128)}), f32[64,16,128]{2,1,0:T(8,128)S(1)}, u32[]{:S(2)}, u32[]{:S(2)}) %all-to-all-start.4) | async-done | bytes 524320 | tf_op jit(solution)/shard_map/all_to_all | solution.py:120
  222.6 1.0 copy.90
  (44 shorter events, 10.1 us)
Async XLA Ops:
  0.6 3.1 %copy-start = (bf16[512,1024]{1,0:T(8,128)(2,1)S(1)}, bf16[512,1024]{1,0:T(8,128)(2,1)}, u32[]{:S(2)}) copy-start(bf16[512,1024]{1,0:T(8,128)(2,1)} %param.14) | copy-start | bytes 3145732
  23.5 41.5 %all-to-all-start = ((bf16[1,2,256,1024]{3,1,0,2:T(2,128)(2,1)}), bf16[1,2,256,1024]{3,1,0,2:T(2,128)(2,1)S(1)}, u32[]{:S(2)}, u32[]{:S(2)}) async-start(bf16[1,2,256,1024]{3,1,0,2:T(2,128)(2,1)} %bitcast.197), calls=%async_computation | async-start | bytes 2097152 | tf_op jit(solution)/shard_map/all_to_all | solution.py:77
  98.0 34.7 %all-to-all-start.1 = ((bf16[1,128,4,1024]{3,2,0,1:T(4,128)(2,1)}), bf16[1,128,4,1024]{3,2,0,1:T(4,128)(2,1)S(1)}, u32[]{:S(2)}, u32[]{:S(2)}) async-start(bf16[1,128,4,1024]{3,2,0,1:T(4,128)(2,1)} %bitcast.198), calls=%async_computation.1 | async-start | bytes 2097152 | tf_op jit(solution)/shard_map/all_to_all | solution.py:90
  161.9 26.3 %copy-start.1 = (s32[1,256]{1,0:T(1,128)S(1)}, s32[1,256]{1,0:T(1,128)}, u32[]{:S(2)}) copy-start(s32[1,256]{1,0:T(1,128)} %param.17) | copy-start | bytes 3076
  164.6 23.5 %all-to-all-start.2 = ((bf16[64,16,256]{2,1,0:T(8,128)(2,1)}), bf16[64,16,256]{2,1,0:T(8,128)(2,1)S(1)}, u32[]{:S(2)}, u32[]{:S(2)}) async-start(bf16[64,16,256]{2,1,0:T(8,128)(2,1)} %bitcast.24), calls=%async_computation.2 | async-start | bytes 1048576 | tf_op jit(solution)/shard_map/all_to_all | solution.py:106
  197.6 25.0 %all-to-all-start.4 = ((f32[64,16,128]{2,1,0:T(8,128)}), f32[64,16,128]{2,1,0:T(8,128)S(1)}, u32[]{:S(2)}, u32[]{:S(2)}) async-start(f32[64,16,128]{2,1,0:T(8,128)} %stack.2), calls=%async_computation.4 | async-start | bytes 1048576 | tf_op jit(solution)/shard_map/all_to_all | solution.py:120
